TPU v7x, 256 devices: a whole 4x4x8 slice. The times are simulated.
256 devices in a mesh: row: 8 (over z), col: 32 (over y, x, core).
Axes of the slice: x: 4, y: 4, z: 8, core: 2. Of those that a mesh axis runs over, the one named last changes fastest.
Arguments:
- matrix: float32 [16384, 16384], P('row', 'col'), may hold values from -48 to 48, as said below
- pivots: int32 [2, 64], replicated, may hold values from 128 to 16383, as said below
Outputs:
- factored: float32 [16384, 16384], P('row', 'col')
Inputs may be any that keep to these rules, and one draw needn't show every extreme that they name: `pivots`: the 128 entries are distinct global row numbers. `matrix`: the entry of row pivots[c, k] in global column c * 64 + k dominates the other entries of its global column, so that multipliers stay well below one.
All inputs are finite; a program needn't handle non-finite values.
Results may differ from a plain program's by a relative error of at most 0.0002.
Values sent between devices are 32-bit elements; how exact they have to be, the bound alone decides.
A program may use at most 64 MiB of HBM per device.

v0:
```python
import jax
import jax.numpy as jnp
from jax import lax
from jax.sharding import PartitionSpec as P

NB = 64
HIGHEST_PRECISION = lax.Precision.HIGHEST


def from_root(value, axis, source):
    kept = jnp.where(lax.axis_index(axis) == source, value, 0).astype(value.dtype)
    return lax.psum(kept, axis)


def eliminate(panel_t):
    panel_width, row_count = panel_t.shape
    row_ids = jnp.arange(row_count, dtype=jnp.int32)
    col_ids = jnp.arange(panel_width, dtype=jnp.int32)

    def eliminate_step(column, current):
        pivot_line = lax.dynamic_index_in_dim(current, column, 1, keepdims=False)
        pivot_value = lax.dynamic_index_in_dim(pivot_line, column, 0, keepdims=False)
        weight = 1.0 / pivot_value
        column_line = lax.dynamic_index_in_dim(current, column, 0, keepdims=False)
        below_rows = row_ids > column
        multiplier = jnp.where(below_rows, column_line * weight, 0.0)
        later_part = jnp.where(col_ids > column, pivot_line, 0.0)
        current = current - later_part[:, None] * multiplier[None, :]
        return jnp.where(
            (col_ids == column)[:, None] & below_rows[None, :], multiplier[None, :], current
        )

    return lax.fori_loop(0, panel_width, eliminate_step, panel_t)


def solve_rows(top_t, right_side):
    unit_part = jnp.tril(top_t.T, -1) + jnp.eye(top_t.shape[0], dtype=top_t.dtype)
    return lax.linalg.triangular_solve(
        unit_part, right_side, left_side=True, lower=True, unit_diagonal=True
    )


def fetch_rows(local_matrix, global_rows, my_row, grid_rows):
    block_ids = global_rows // NB
    owned = block_ids % grid_rows == my_row
    local_index = block_ids // grid_rows * NB + global_rows % NB
    row_values = jnp.where(owned[:, None], local_matrix[jnp.where(owned, local_index, 0)], 0.0)
    return (row_values, jnp.where(owned, local_index, local_matrix.shape[0]))


def place_rows(local_matrix, local_index, row_values):
    return local_matrix.at[local_index].set(row_values, mode="drop")


def apply_panel(
    local_matrix,
    panel,
    lower_t,
    top_t,
    upper_rows,
    row_blocks,
    col_blocks,
    my_row,
    my_col,
    grid_rows,
    grid_cols,
):
    below_rows = row_blocks > panel
    right_cols = col_blocks > panel
    product = lax.dot_general(
        lower_t,
        upper_rows,
        (((0,), (0,)), ((), ())),
        precision=HIGHEST_PRECISION,
        preferred_element_type=jnp.float32,
    )
    result = jnp.where(
        below_rows[:, None] & right_cols[None, :], local_matrix - product, local_matrix
    )
    col_start = panel // grid_cols * NB
    row_start = panel // grid_rows * NB
    owns_col = my_col == panel % grid_cols
    owns_row = my_row == panel % grid_rows
    col_part = jnp.where(
        below_rows[:, None] & owns_col, lower_t.T, result[:, col_start : col_start + NB]
    )
    result = result.at[:, col_start : col_start + NB].set(col_part)
    row_part = jnp.where(
        right_cols[None, :] & owns_row, upper_rows, result[row_start : row_start + NB]
    )
    result = result.at[row_start : row_start + NB].set(row_part)
    corner = jnp.where(
        owns_row & owns_col, top_t.T, result[row_start : row_start + NB, col_start : col_start + NB]
    )
    return result.at[row_start : row_start + NB, col_start : col_start + NB].set(corner)


def shards(matrix, pivots):
    rows_dev, cols_dev = matrix.shape
    grid_rows = lax.axis_size("row")
    grid_cols = lax.axis_size("col")
    my_row = lax.axis_index("row")
    my_col = lax.axis_index("col")
    row_blocks = jnp.arange(rows_dev, dtype=jnp.int32) // NB * grid_rows + my_row
    col_blocks = jnp.arange(cols_dev, dtype=jnp.int32) // NB * grid_cols + my_col
    local_matrix = matrix
    for panel in range(2):
        top_global = panel * NB + jnp.arange(NB, dtype=jnp.int32)
        pivot_values, pivot_index = fetch_rows(local_matrix, pivots[panel], my_row, grid_rows)
        top_values, top_index = fetch_rows(local_matrix, top_global, my_row, grid_rows)
        new_top, new_pivot = lax.psum((pivot_values, top_values), "row")
        local_matrix = place_rows(
            place_rows(local_matrix, top_index, new_top), pivot_index, new_pivot
        )
        col_start = panel // grid_cols * NB
        panel_t = jnp.concatenate(
            [
                new_top[:, col_start : col_start + NB].T,
                local_matrix[:, col_start : col_start + NB].T,
            ],
            axis=1,
        )
        factored_panel = eliminate(panel_t)
        lower_t, top_t = (
            from_root(factored_panel[:, NB:], "col", panel % grid_cols),
            from_root(factored_panel[:, :NB], "col", panel % grid_cols),
        )
        upper_rows = solve_rows(top_t, new_top)
        local_matrix = apply_panel(
            local_matrix,
            panel,
            lower_t,
            top_t,
            upper_rows,
            row_blocks,
            col_blocks,
            my_row,
            my_col,
            grid_rows,
            grid_cols,
        )
    return local_matrix


def solution(mesh):
    placed = (P("row", "col"), P())
    return jax.shard_map(
        shards, mesh=mesh, in_specs=placed, out_specs=P("row", "col"), check_vma=False
    )
```

profile of v0, /device:TPU:1, one launch (start us, length us, event | category | flops | bytes accessed | tf_op | source)
XLA Modules:
  0.0 983.9 jit_solution(361981040310378852)
XLA Ops:
  6.5 4.7 copy.48
  11.3 2.9 gather_fusion.1
  14.2 2.9 gather_fusion
  17.1 0.7 broadcast_select_fusion.2
  17.8 0.7 broadcast_select_fusion.3
  18.8 0.7 compare_reduce_fusion
  19.5 70.9 %all-reduce.13.cloned.1.call-done = (f32[64,512]{1,0:T(8,128)}, f32[64,512]{1,0:T(8,128)}) async-done(((f32[64,512]{1,0:T(8,128)}, f32[64,512]{1,0:T(8,128)}), (f32[64,512]{1,0:T(8,128)}, f32[64,512]{1,0:T(8,128)})) %all-reduce.13.cloned.1.call-update) | async-done | bytes 262160 | tf_op jit(solution)/shard_map/psum | solution.py:111
  90.5 0.8 slice_bitcast_fusion.3
  91.2 5.3 scatter_fusion
  96.6 5.3 scatter_fusion.1
  101.9 1.3 slice_bitcast_fusion.1
  103.6 133.3 %while.42 = (s32[]{:T(128)}, f32[64,2112]{1,0:T(8,128)S(1)}, s32[]{:T(128)}, f32[1,1]{1,0:T(1,128)}, s32[]{:T(128)}, /*index=5*/s32[]{:T(128)}, s32[]{:T(128)}) while((s32[]{:T(128)}, f32[64,2112]{1,0:T(8,128)S(1)}, s32[]{:T(128)}, f32[1,1]{1,0:T(1,128)}, s32[]{:T(128)}, /*index=5*/s32[]{:T(128)}, s32[]{:T(128)}) %tuple.126), condition=%wide.region_5.6_spmd.clone.clone, body=%wide.region_4.5_spmd.clone.clone.sunk | while | flops 547205 | bytes 2196437 | solution.py:33
  103.6 0.7 dynamic_slice.81
  105.7 0.7 dynamic_slice.81
  107.8 0.7 dynamic_slice.81
  109.9 0.7 dynamic_slice.81
  111.9 0.7 dynamic_slice.81
  114.0 0.7 dynamic_slice.81
  237.3 1.1 slice_select_fusion.1
  238.4 123.9 %psum.59 = f32[64,64]{1,0:T(8,128)S(1)} all-reduce(f32[64,64]{1,0:T(8,128)S(1)} %fusion.17), channel_id=1, replica_groups=mesh['row'=8,'col'=32] {'col'}, use_global_device_ids=true, to_apply=%region_7.8 | all-reduce | flops 4096 | bytes 32768 | tf_op jit(solution)/shard_map/psum | solution.py:12
  362.5 4.9 custom-call.4
  367.7 108.8 %all-reduce.7.cloned.1.call-done = f32[64,2048]{0,1:T(8,128)} async-done(((f32[64,2048]{0,1:T(8,128)}), f32[64,2048]{0,1:T(8,128)}) %all-reduce.7.cloned.1.call-update) | async-done | bytes 524304 | tf_op jit(solution)/shard_map/psum | solution.py:12
  476.5 6.4 subtract_select_fusion.3
  483.0 2.0 copy-done
  485.0 1.0 select_select_fusion.1
  486.0 5.8 scatter.60
  491.8 1.6 constant_dynamic-update-slice_fusion.1
  493.4 2.8 scatter.62
  496.2 2.9 gather_fusion.3
  499.1 2.9 gather_fusion.2
  502.0 0.7 broadcast_select_fusion
  502.8 0.7 broadcast_select_fusion.1
  503.6 67.8 %all-reduce.11.cloned.1.call-done = (f32[64,512]{1,0:T(8,128)}, f32[64,512]{1,0:T(8,128)}) async-done(((f32[64,512]{1,0:T(8,128)}, f32[64,512]{1,0:T(8,128)}), (f32[64,512]{1,0:T(8,128)}, f32[64,512]{1,0:T(8,128)})) %all-reduce.11.cloned.1.call-update) | async-done | bytes 262160 | tf_op jit(solution)/shard_map/psum | solution.py:111
  571.5 0.8 slice_bitcast_fusion.2
  572.2 5.3 scatter_fusion.2
  577.5 5.3 scatter_fusion.3
  582.9 1.3 slice_bitcast_fusion
  584.6 133.3 %while.43 = (s32[]{:T(128)}, f32[64,2112]{1,0:T(8,128)S(1)}, s32[]{:T(128)}, f32[1,1]{1,0:T(1,128)}, s32[]{:T(128)}, /*index=5*/s32[]{:T(128)}, s32[]{:T(128)}) while((s32[]{:T(128)}, f32[64,2112]{1,0:T(8,128)S(1)}, s32[]{:T(128)}, f32[1,1]{1,0:T(1,128)}, s32[]{:T(128)}, /*index=5*/s32[]{:T(128)}, s32[]{:T(128)}) %tuple.129), condition=%wide.region_14.16_spmd.clone.clone, body=%wide.region_13.15_spmd.clone.clone.sunk | while | flops 547205 | bytes 2196437 | solution.py:33
  718.3 1.1 slice_select_fusion
  719.4 124.1 %psum.63 = f32[64,64]{1,0:T(8,128)S(1)} all-reduce(f32[64,64]{1,0:T(8,128)S(1)} %fusion.16), channel_id=1, replica_groups=mesh['row'=8,'col'=32] {'col'}, use_global_device_ids=true, to_apply=%region_16.18 | all-reduce | flops 4096 | bytes 32768 | tf_op jit(solution)/shard_map/psum | solution.py:12
  843.6 4.9 custom-call.5
  848.9 108.8 %all-reduce.9.cloned.1.call-done = f32[64,2048]{0,1:T(8,128)} async-done(((f32[64,2048]{0,1:T(8,128)}), f32[64,2048]{0,1:T(8,128)}) %all-reduce.9.cloned.1.call-update) | async-done | bytes 524304 | tf_op jit(solution)/shard_map/psum | solution.py:12
  957.7 6.4 subtract_select_fusion.2
  964.1 2.0 copy-done.1
  966.2 1.0 select_select_fusion
  967.2 5.8 scatter.65
  973.0 1.6 constant_dynamic-update-slice_fusion
  974.6 2.8 scatter.67
  (943 shorter events, 164.5 us)
Async XLA Ops:
  6.5 4.7 copy-start.6
  6.5 83.9 %all-reduce.13.cloned.1.call-start = ((), (), s32[]{:S(2)}) async-start(), calls=%async_computation.3 | async-start | bytes 524288 | tf_op jit(solution)/shard_map/psum | solution.py:111
  18.6 457.9 %all-reduce.7.cloned.1.call-start = ((), (), s32[]{:S(2)}) async-start(), calls=%async_computation | async-start | bytes 2097152 | tf_op jit(solution)/shard_map/psum | solution.py:12
  236.9 130.5 %copy-start.4 = (f32[64,512]{1,0:T(8,128)S(1)}, f32[64,512]{1,0:T(8,128)}, u32[]{:S(2)}) copy-start(f32[64,512]{1,0:T(8,128)} %get-tuple-element.386) | copy-start | bytes 393220
  362.4 209.1 %all-reduce.11.cloned.1.call-start = ((), (), s32[]{:S(2)}) async-start(), calls=%async_computation.2 | async-start | bytes 524288 | tf_op jit(solution)/shard_map/psum | solution.py:111
  476.5 8.5 copy-start.2
  483.0 2.0 copy-start
  503.5 454.2 %all-reduce.9.cloned.1.call-start = ((), (), s32[]{:S(2)}) async-start(), calls=%async_computation.1 | async-start | bytes 2097152 | tf_op jit(solution)/shard_map/psum | solution.py:12
  717.9 130.6 %copy-start.5 = (f32[64,512]{1,0:T(8,128)S(1)}, f32[64,512]{1,0:T(8,128)}, u32[]{:S(2)}) copy-start(f32[64,512]{1,0:T(8,128)} %get-tuple-element.384) | copy-start | bytes 393220
  957.7 8.4 copy-start.3
  964.1 2.0 copy-start.1
Sparse Core Ops, SparseCore 0:
  18.7 71.6 all-reduce.12
  362.5 113.9 all-reduce.6
  503.6 67.7 all-reduce.10
  843.7 113.9 all-reduce.8
where the time goes:
time: 987 us; the launch traced here: 984 us
  waiting for transfers between devices  356 us (36%)
  blocking collectives  248 us (25%)
  local copies, waits for them, and re-layouts  195 us (20%)
  loops' own time  101 us (10%)
  other arithmetic  56.1 us (6%)
  matrix products  13.5 us (1%)
  between operations  13.4 us (1%)
    psum x2, blocking collectives, from_root(): return lax.psum(kept, axis)  248 us
    psum x2, waiting for transfers between devices, from_root(): return lax.psum(kept, axis)  218 us
    psum x2, waiting for transfers between devices, shards(): new_top, new_pivot = lax.psum((pivot_values, top_values), 'row')  139 us
    another operation x2, loops' own time, eliminate(): return lax.fori_loop(0, panel_width, eliminate_step, panel_t)  101 us
    dynamic_slice x128, local copies, waits for them, and re-layouts, eliminate_step(): lax.dynamic_index_in_dim(pivot_line, column, 0, keepdims=False)  85.8 us
    while x128, local copies, waits for them, and re-layouts  45.2 us
    select_n x128, other arithmetic, eliminate_step(): jnp.where((col_ids == column)[:, None] & below_rows[None, :], multiplier[...  25.8 us
    scatter x4, local copies, waits for them, and re-layouts, place_rows(): return local_matrix.at[local_index].set(row_values, mode='drop')  21.3 us
  transfers between devices with their start and end apart: 4, of which 4 were waited for; matrix products, arithmetic and copies ran while one was open for 1% of the time, Pallas kernels for 0%

commit v1 on v0

--- a/solution.py
+++ b/solution.py
@@ -9,7 +9,7 @@
 
 def from_root(value, axis, source):
     kept = jnp.where(lax.axis_index(axis) == source, value, 0).astype(value.dtype)
-    return lax.psum(kept, axis)
+    return lax.all_gather(kept, axis).sum(axis=0)
 
 
 def eliminate(panel_t):

time: 987 us -> 687 us (0.70)
  blocking collectives: 248 us -> 64.1 us
  waiting for transfers between devices: 356 us -> 228 us
  other arithmetic: 56.1 us -> 69.7 us
    psum x2 -> x0, blocking collectives: 248 us -> none  [from_root(): return lax.psum(kept, axis)]
    psum x2 -> x0, waiting for transfers between devices: 218 us -> none  [from_root(): return lax.psum(kept, axis)]
    all_gather x0 -> x2, waiting for transfers between devices: none -> 88.9 us  [from_root(): return lax.all_gather(kept, axis).sum(axis=0)]
    all_gather x0 -> x2, blocking collectives: none -> 64.1 us  [from_root(): return lax.all_gather(kept, axis).sum(axis=0)]
    reduce_sum x0 -> x4, other arithmetic: none -> 14 us  [from_root(): return lax.all_gather(kept, axis).sum(axis=0)]
    while x130 -> x128, local copies, waits for them, and re-layouts: 45.9 us -> 45.2 us
  transfers between devices with their start and end apart: 4 -> 4, of which waited for: 4 -> 4; matrix products, arithmetic and copies ran while one was open for 1% -> 2% of each run, Pallas kernels for 0% -> 0%
where the time goes in v1:
time: 687 us; the launch traced here: 684 us
  waiting for transfers between devices  228 us (33%)
  local copies, waits for them, and re-layouts  195 us (28%)
  loops' own time  101 us (15%)
  other arithmetic  69.7 us (10%)
  blocking collectives  64.1 us (9%)
  between operations  13.5 us (2%)
  matrix products  12 us (2%)
    psum x2, waiting for transfers between devices, shards(): new_top, new_pivot = lax.psum((pivot_values, top_values), 'row')  139 us
    another operation x2, loops' own time, eliminate(): return lax.fori_loop(0, panel_width, eliminate_step, panel_t)  101 us
    all_gather x2, waiting for transfers between devices, from_root(): return lax.all_gather(kept, axis).sum(axis=0)  88.9 us
    dynamic_slice x128, local copies, waits for them, and re-layouts, eliminate_step(): lax.dynamic_index_in_dim(pivot_line, column, 0, keepdims=False)  85.8 us
    all_gather x2, blocking collectives, from_root(): return lax.all_gather(kept, axis).sum(axis=0)  64.1 us
    while x128, local copies, waits for them, and re-layouts  45.2 us
    select_n x128, other arithmetic, eliminate_step(): jnp.where((col_ids == column)[:, None] & below_rows[None, :], multiplier[...  25.8 us
    scatter x4, local copies, waits for them, and re-layouts, place_rows(): return local_matrix.at[local_index].set(row_values, mode='drop')  21.3 us
  transfers between devices with their start and end apart: 4, of which 4 were waited for; matrix products, arithmetic and copies ran while one was open for 2% of the time, Pallas kernels for 0%

profile of v1, /device:TPU:1, one launch (start us, length us, event | category | flops | bytes accessed | tf_op | source)
XLA Modules:
  0.0 683.8 jit_solution(73516974612721246)
XLA Ops:
  6.5 4.7 copy.48
  11.3 2.9 gather_fusion.1
  14.2 2.9 gather_fusion
  17.1 0.7 broadcast_select_fusion.2
  17.8 0.7 broadcast_select_fusion.3
  18.7 71.8 %all-reduce.7.cloned.1.call-done = (f32[64,512]{1,0:T(8,128)}, f32[64,512]{1,0:T(8,128)}) async-done(((f32[64,512]{1,0:T(8,128)}, f32[64,512]{1,0:T(8,128)}), (f32[64,512]{1,0:T(8,128)}, f32[64,512]{1,0:T(8,128)})) %all-reduce.7.cloned.1.call-update) | async-done | bytes 262160 | tf_op jit(solution)/shard_map/psum | solution.py:111
  90.5 0.8 slice_bitcast_fusion.3
  91.2 5.3 scatter_fusion
  96.6 5.3 scatter_fusion.1
  101.9 1.3 slice_bitcast_fusion.1
  103.6 133.3 %while.42 = (s32[]{:T(128)}, f32[64,2112]{1,0:T(8,128)S(1)}, s32[]{:T(128)}, f32[1,1]{1,0:T(1,128)}, s32[]{:T(128)}, /*index=5*/s32[]{:T(128)}, s32[]{:T(128)}) while((s32[]{:T(128)}, f32[64,2112]{1,0:T(8,128)S(1)}, s32[]{:T(128)}, f32[1,1]{1,0:T(1,128)}, s32[]{:T(128)}, /*index=5*/s32[]{:T(128)}, s32[]{:T(128)}) %tuple.128), condition=%wide.region_5.6_spmd.clone.clone, body=%wide.region_4.5_spmd.clone.clone.sunk | while | flops 547205 | bytes 2196437 | solution.py:33
  103.6 0.7 dynamic_slice.81
  105.7 0.7 dynamic_slice.81
  107.8 0.7 dynamic_slice.81
  109.9 0.7 dynamic_slice.81
  236.9 1.0 slice_select_fusion.1
  238.0 0.7 compare_reduce_fusion
  238.8 31.9 %all-gather.1 = f32[2048,64]{1,0:T(8,128)S(1)} all-gather(f32[64,64]{1,0:T(8,128)S(1)} %slice_select_fusion.7), channel_id=3, replica_groups=mesh['row'=8,'col'=32] {'col'}, dimensions={0}, use_global_device_ids=true | all-gather | bytes 540672 | tf_op jit(solution)/shard_map/all_gather | solution.py:12
  271.0 4.9 custom-call.4
  276.3 44.1 %all-gather.7.cloned.1.call-done = f32[2048,2048]{1,0:T(8,128)} async-done(((f32[64,2048]{1,0:T(8,128)}), f32[2048,2048]{1,0:T(8,128)}) %all-gather.7.cloned.1.call-update) | async-done | bytes 16777232 | tf_op jit(solution)/shard_map/all_gather | solution.py:12
  320.4 6.9 %reduce_sum.36 = f32[64,2048]{1,0:T(8,128)S(1)} reduce(f32[32,64,2048]{2,1,0:T(8,128)} %bitcast.138, f32[]{:T(128)} %constant.578.clone.1), dimensions={0}, to_apply=%region_6.7 | reduce | flops 4063232 | bytes 17301508 | tf_op jit(solution)/shard_map/reduce_sum | solution.py:12
  327.6 5.7 subtract_select_fusion.3
  333.3 2.0 copy-done
  335.3 1.0 select_select_fusion.1
  336.3 5.8 scatter.60
  342.1 1.6 constant_dynamic-update-slice_fusion.1
  343.7 2.8 scatter.62
  346.5 2.9 gather_fusion.3
  349.4 2.9 gather_fusion.2
  352.3 0.7 broadcast_select_fusion
  353.1 0.7 broadcast_select_fusion.1
  353.9 67.2 %all-reduce.5.cloned.1.call-done = (f32[64,512]{1,0:T(8,128)}, f32[64,512]{1,0:T(8,128)}) async-done(((f32[64,512]{1,0:T(8,128)}, f32[64,512]{1,0:T(8,128)}), (f32[64,512]{1,0:T(8,128)}, f32[64,512]{1,0:T(8,128)})) %all-reduce.5.cloned.1.call-update) | async-done | bytes 262160 | tf_op jit(solution)/shard_map/psum | solution.py:111
  421.0 0.8 slice_bitcast_fusion.2
  421.8 5.3 scatter_fusion.2
  427.1 5.3 scatter_fusion.3
  432.5 1.3 slice_bitcast_fusion
  434.2 133.3 %while.43 = (s32[]{:T(128)}, f32[64,2112]{1,0:T(8,128)S(1)}, s32[]{:T(128)}, f32[1,1]{1,0:T(1,128)}, s32[]{:T(128)}, /*index=5*/s32[]{:T(128)}, s32[]{:T(128)}) while((s32[]{:T(128)}, f32[64,2112]{1,0:T(8,128)S(1)}, s32[]{:T(128)}, f32[1,1]{1,0:T(1,128)}, s32[]{:T(128)}, /*index=5*/s32[]{:T(128)}, s32[]{:T(128)}) %tuple.131), condition=%wide.region_14.16_spmd.clone.clone, body=%wide.region_13.15_spmd.clone.clone.sunk | while | flops 547205 | bytes 2196437 | solution.py:33
  567.5 1.0 slice_select_fusion
  568.6 32.2 %all-gather.3 = f32[2048,64]{1,0:T(8,128)S(1)} all-gather(f32[64,64]{1,0:T(8,128)S(1)} %slice_select_fusion.6), channel_id=5, replica_groups=mesh['row'=8,'col'=32] {'col'}, dimensions={0}, use_global_device_ids=true | all-gather | bytes 540672 | tf_op jit(solution)/shard_map/all_gather | solution.py:12
  601.1 4.9 custom-call.5
  606.3 44.8 %all-gather.9.cloned.1.call-done = f32[2048,2048]{1,0:T(8,128)} async-done(((f32[64,2048]{1,0:T(8,128)}), f32[2048,2048]{1,0:T(8,128)}) %all-gather.9.cloned.1.call-update) | async-done | bytes 16777232 | tf_op jit(solution)/shard_map/all_gather | solution.py:12
  651.1 6.9 %reduce_sum.38 = f32[64,2048]{1,0:T(8,128)S(1)} reduce(f32[32,64,2048]{2,1,0:T(8,128)} %bitcast.139, f32[]{:T(128)} %constant.578.clone.1), dimensions={0}, to_apply=%region_15.17 | reduce | flops 4063232 | bytes 17301508 | tf_op jit(solution)/shard_map/reduce_sum | solution.py:12
  658.4 5.7 subtract_select_fusion.2
  664.1 2.0 copy-done.1
  666.1 1.0 select_select_fusion
  667.1 5.8 scatter.65
  672.9 1.6 constant_dynamic-update-slice_fusion
  674.5 2.8 scatter.67
  (945 shorter events, 166.1 us)
Async XLA Ops:
  6.5 4.7 copy-start.4
  6.5 83.9 %all-reduce.7.cloned.1.call-start = ((), (), s32[]{:S(2)}) async-start(), calls=%async_computation.3 | async-start | bytes 524288 | tf_op jit(solution)/shard_map/psum | solution.py:111
  18.6 301.8 %all-gather.7.cloned.1.call-start = ((), (), s32[]{:S(2)}) async-start(), calls=%async_computation | async-start | bytes 17301504 | tf_op jit(solution)/shard_map/all_gather | solution.py:12
  103.6 172.3 %copy-start.2 = (f32[64,512]{1,0:T(8,128)S(1)}, f32[64,512]{1,0:T(8,128)}, u32[]{:S(2)}) copy-start(f32[64,512]{1,0:T(8,128)} %get-tuple-element.390) | copy-start | bytes 393220
  238.0 183.1 %all-reduce.5.cloned.1.call-start = ((), (), s32[]{:S(2)}) async-start(), calls=%async_computation.2 | async-start | bytes 524288 | tf_op jit(solution)/shard_map/psum | solution.py:111
  333.3 2.0 copy-start
  353.8 297.3 %all-gather.9.cloned.1.call-start = ((), (), s32[]{:S(2)}) async-start(), calls=%async_computation.1 | async-start | bytes 17301504 | tf_op jit(solution)/shard_map/all_gather | solution.py:12
  434.2 171.8 %copy-start.3 = (f32[64,512]{1,0:T(8,128)S(1)}, f32[64,512]{1,0:T(8,128)}, u32[]{:S(2)}) copy-start(f32[64,512]{1,0:T(8,128)} %get-tuple-element.388) | copy-start | bytes 393220
  664.1 2.0 copy-start.1
Sparse Core Ops, SparseCore 0:
  18.7 71.6 all-reduce.6
  238.1 82.2 all-gather.6
  353.9 67.0 all-reduce.4
  568.7 82.4 all-gather.8
